TPU v7x, 512 devices: a whole 4x8x8 slice. The times are simulated.
512 devices in a mesh: ens: 32 (over z, y_lo, core), pen: 16 (over x, y_hi).
Axes of the slice: x: 4, y: 8 (y_hi: 4, y_lo: 2; y = y_hi * 2 + y_lo), z: 8, core: 2. Of those that a mesh axis runs over, the one named last changes fastest.
Arguments:
- state: float32 [2, 32, 4, 256, 512], P(None, 'ens', None, 'pen'), may hold values from -8 to 8, as said below
- accum: float32 [2, 32, 4, 256, 512], P(None, 'ens', None, 'pen'), may hold values from -8 to 8, as said below
- base_flow: float32 [6, 4, 256, 256], P(None, None, 'pen', 'ens'), may hold values from -6 to 6
Outputs:
- state_next: float32 [2, 32, 4, 256, 512], P(None, 'ens', None, 'pen')
- accum_next: float32 [2, 32, 4, 256, 512], P(None, 'ens', None, 'pen')
Inputs may be any that keep to these rules, and one draw needn't show every extreme that they name: `state`: each field of each perturbation and level is the spectrum of a real field: the entry at ((256 - ky) mod 256, (256 - kx) mod 256) is the complex conjugate of the entry at (ky, kx). `accum`: each field of each perturbation and level is the spectrum of a real field: the entry at ((256 - ky) mod 256, (256 - kx) mod 256) is the complex conjugate of the entry at (ky, kx).
All inputs are finite; a program needn't handle non-finite values.
Results may differ from a plain program's by a relative error of at most 0.0003.
Values sent between devices are 32-bit elements; how exact they have to be, the bound alone decides.
A program may use at most 64 MiB of HBM per device.

v0:
```python
import math
import jax
import jax.numpy as jnp
from jax import lax
from jax.sharding import PartitionSpec as P

viscosity = 0.05
diffusivity = 0.05
vertical_mixing = 0.5
buoyancy_gain = 0.5
stratification = 0.5
memory_factor = -5.0 / 9.0
weight_factor = 15.0 / 16.0
time_step = 0.4


def wave_numbers(amount, offset, length):
    position = offset + jnp.arange(amount, dtype=jnp.int32)
    half_length = length // 2
    signed = jnp.where(position <= half_length, position, position - length)
    derivative = jnp.where(position == half_length, 0, signed)
    return (2.0 * math.pi / length * derivative.astype(jnp.float32), signed)


def times_i(real_part, imag_part, factor):
    return (-factor * imag_part, factor * real_part)


def vertical(quantity, level_axis):
    depth = quantity.shape[level_axis]
    lower = lax.slice_in_dim(quantity, 0, 1, axis=level_axis)
    upper = lax.slice_in_dim(quantity, depth - 1, depth, axis=level_axis)
    padded = jnp.concatenate([lower, quantity, upper], axis=level_axis)
    above = lax.slice_in_dim(padded, 2, depth + 2, axis=level_axis)
    below = lax.slice_in_dim(padded, 0, depth, axis=level_axis)
    return above + below - 2.0 * quantity


def tendency(vort, buoy, advect, across, kappa_x, square, level_axis):
    tend_vort_re = (
        -advect[0]
        + buoyancy_gain * (-kappa_x * buoy[1])
        - viscosity * square * vort[0]
        + vertical_mixing * vertical(vort[0], level_axis)
    )
    tend_vort_im = (
        -advect[1]
        + buoyancy_gain * (kappa_x * buoy[0])
        - viscosity * square * vort[1]
        + vertical_mixing * vertical(vort[1], level_axis)
    )
    tend_buoy_re = (
        -advect[2]
        - stratification * across[0]
        - diffusivity * square * buoy[0]
        + vertical_mixing * vertical(buoy[0], level_axis)
    )
    tend_buoy_im = (
        -advect[3]
        - stratification * across[1]
        - diffusivity * square * buoy[1]
        + vertical_mixing * vertical(buoy[1], level_axis)
    )
    return jnp.stack(
        [
            jnp.concatenate([tend_vort_re, tend_vort_im], axis=-1),
            jnp.concatenate([tend_buoy_re, tend_buoy_im], axis=-1),
        ]
    )


def dft_tables(length):
    position = jnp.arange(length, dtype=jnp.int32)
    product = position[:, None] * position[None, :] % length
    angle = 2.0 * math.pi / length * product.astype(jnp.float32)
    scale = 1.0 / math.sqrt(length)
    return (scale * jnp.cos(angle), scale * jnp.sin(angle))


def to_physical(spectral, x_table, y_table):
    mixed_space = jnp.einsum(
        "fplkj,jcx->fplcxk", spectral, x_table, precision=lax.Precision.HIGHEST
    )
    return jnp.einsum(
        "fplcxk,ckm->fplxm",
        lax.all_to_all(mixed_space, "pen", split_axis=4, concat_axis=5, tiled=True),
        y_table,
        precision=lax.Precision.HIGHEST,
    )


def on_device(state, accum, base_flow):
    grid_size = state.shape[-1] // 2
    row_count = state.shape[3]
    base_all = lax.all_gather(base_flow, "ens", axis=3, tiled=True)
    kappa_rows, signed_y = wave_numbers(row_count, lax.axis_index("pen") * row_count, grid_size)
    kappa_cols, signed_x = wave_numbers(grid_size, 0, grid_size)
    kappa_y = kappa_rows[:, None]
    kappa_x = kappa_cols[None, :]
    wave_square = signed_y[:, None] ** 2 + signed_x[None, :] ** 2
    factor = (2.0 * math.pi / grid_size) ** 2
    square = factor * wave_square.astype(jnp.float32)
    inverse = jnp.where(
        wave_square > 0, 1.0 / (factor * jnp.maximum(wave_square, 1).astype(jnp.float32)), 0.0
    )
    vort = (state[0][..., :grid_size], state[0][..., grid_size:])
    buoy = (state[1][..., :grid_size], state[1][..., grid_size:])
    potential_re = -vort[0] * inverse
    potential_im = -vort[1] * inverse
    flow_x = times_i(potential_re, potential_im, -kappa_y)
    flow_y = times_i(potential_re, potential_im, kappa_x)
    vort_x = times_i(vort[0], vort[1], kappa_x)
    vort_y = times_i(vort[0], vort[1], kappa_y)
    buoy_x = times_i(buoy[0], buoy[1], kappa_x)
    buoy_y = times_i(buoy[0], buoy[1], kappa_y)
    cosine_table, sine_table = dft_tables(grid_size)
    x_table = jnp.concatenate(
        [
            jnp.stack([cosine_table, sine_table], axis=1),
            jnp.stack([-sine_table, cosine_table], axis=1),
        ],
        axis=0,
    )
    y_table = jnp.stack([cosine_table, -sine_table])
    components = [flow_x, flow_y, vort_x, vort_y, buoy_x, buoy_y]
    spectral = jnp.stack([jnp.concatenate(component, axis=-1) for component in components])
    physical = to_physical(spectral, x_table, y_table)
    flow_x_p, flow_y_p = (physical[0], physical[1])
    vort_x_p, vort_y_p = (physical[2], physical[3])
    buoy_x_p, buoy_y_p = (physical[4], physical[5])
    advect_vort = (
        base_all[0] * vort_x_p
        + base_all[1] * vort_y_p
        + flow_x_p * base_all[2]
        + flow_y_p * base_all[3]
    )
    advect_buoy = (
        base_all[0] * buoy_x_p
        + base_all[1] * buoy_y_p
        + flow_x_p * base_all[4]
        + flow_y_p * base_all[5]
    )
    advect_both = jnp.stack([advect_vort, advect_buoy])
    y_forward = jnp.stack([cosine_table, -sine_table], axis=1)
    x_forward = jnp.stack(
        [
            jnp.concatenate([cosine_table, -sine_table], axis=1),
            jnp.concatenate([sine_table, cosine_table], axis=1),
        ]
    )
    spread = jnp.einsum(
        "fplxy,yck->fplckx", advect_both, y_forward, precision=lax.Precision.HIGHEST
    )
    spectra = jnp.einsum(
        "fplckx,cxm->fplkm",
        lax.all_to_all(spread, "pen", split_axis=4, concat_axis=5, tiled=True),
        x_forward,
        precision=lax.Precision.HIGHEST,
    )
    advect = (
        spectra[0][..., :grid_size],
        spectra[0][..., grid_size:],
        spectra[1][..., :grid_size],
        spectra[1][..., grid_size:],
    )
    tend = tendency(vort, buoy, advect, flow_y, kappa_x, square, 1)
    accum_next = memory_factor * accum + tend
    state_next = state + weight_factor * time_step * accum_next
    return (state_next, accum_next)


def solution(mesh):
    return jax.shard_map(
        on_device,
        mesh=mesh,
        in_specs=(
            P(None, "ens", None, "pen", None),
            P(None, "ens", None, "pen", None),
            P(None, None, "pen", "ens"),
        ),
        out_specs=(P(None, "ens", None, "pen", None), P(None, "ens", None, "pen", None)),
        check_vma=False,
    )
```

profile of v0, /device:TPU:1, one launch (start us, length us, event | category | flops | bytes accessed | tf_op | source)
XLA Modules:
  0.0 172.0 jit_solution(4518188159568962184)
XLA Ops:
  0.7 1.1 sine_multiply_fusion.1
  1.7 1.0 fusion.39
  2.7 1.1 slice_bitcast_fusion.1
  6.5 1.5 convolution_bitcast_fusion
  8.0 5.0 %copy.20 = f32[6,1,4,2,256,16]{5,2,0,3,1,4:T(4,128)} copy(f32[6,1,4,2,256,16]{4,5,2,0,3,1:T(8,128)S(1)} %convolution_bitcast_fusion) | data formatting | bytes 1572864 | tf_op jit(solution)/shard_map/fplkj,jcx->fplcxk/transpose | solution.py:81
  13.0 7.2 %reshape.338 = f32[16,1,12288]{2,1,0:T(1,128)} reshape(f32[256,1,2,6,4,16]{5,4,3,2,1,0:T(4,128)} %bitcast.114) | data formatting | bytes 1572864
  20.2 10.2 %all-to-all-start = ((f32[16,1,12288]{2,1,0:T(1,128)}), f32[16,1,12288]{2,1,0:T(1,128)S(1)}, u32[]{:S(2)}, u32[]{:S(2)}) async-start(f32[16,1,12288]{2,1,0:T(1,128)} %reshape.338), calls=%async_computation | async-start | bytes 1572864 | tf_op jit(solution)/shard_map/all_to_all | solution.py:86
  30.5 71.0 %all_gather.3 = f32[6,4,16,256]{2,1,0,3:T(4,128)S(1)} all-gather(f32[6,4,16,8]{2,1,0,3:T(4,128)S(1)} %copy.13), channel_id=1, replica_groups=mesh['ens'=32,'pen'=16] {'ens'}, dimensions={3}, use_global_device_ids=true | all-gather | bytes 405504 | tf_op jit(solution)/shard_map/all_gather | solution.py:95
  101.4 1.5 fusion.94
  102.9 1.8 %copy.35 = f32[1,4,16,256]{3,2,1,0:T(8,128)} copy(f32[1,4,16,256]{2,1,0,3:T(4,128)} %get-tuple-element.8) | data formatting | bytes 131072
  104.8 1.8 %copy.36 = f32[1,4,16,256]{3,2,1,0:T(8,128)} copy(f32[1,4,16,256]{2,1,0,3:T(4,128)} %get-tuple-element.7) | data formatting | bytes 131072
  106.6 0.8 copy.37
  107.4 0.8 copy.38
  108.6 1.7 fusion.40
  110.3 1.1 multiply_negate_fusion
  111.9 2.4 %reduce = f32[16,12288]{1,0:T(8,128)S(1)} reduce(f32[16,1,12288]{2,1,0:T(1,128)S(1)} %all-to-all-done, f32[]{:T(128)} %broadcast.510), dimensions={1}, to_apply=%all_to_all.22.reduce_sub_computation | reduce | bytes 1572868 | tf_op jit(solution)/shard_map/all_to_all | solution.py:86
  114.3 6.3 %reshape.339 = f32[256,1,2,6,4,16]{5,4,3,2,1,0:T(4,128)} reshape(f32[16,12288]{1,0:T(8,128)S(1)} %reduce) | data formatting | bytes 1572864
  120.6 9.1 %copy.43 = f32[6,1,4,2,16,16,16]{6,4,5,3,2,0,1:T(8,128)} copy(f32[6,1,4,2,16,16,16]{6,2,0,3,5,4,1:T(4,128)} %bitcast.115) | data formatting | bytes 1572864 | tf_op jit(solution)/shard_map/all_to_all | solution.py:86
  129.7 4.9 %reshape.327 = f32[6,4,2,16,256]{4,3,2,1,0:T(8,128)S(1)} reshape(f32[6,1,4,2,16,16,16]{6,5,4,3,2,0,1:T(8,128)} %bitcast.116) | data formatting | bytes 1572864 | tf_op jit(solution)/shard_map/reshape.16
  134.7 0.8 convolution_bitcast_fusion.1
  136.0 1.3 copy.27
  137.3 2.3 %reshape.340 = f32[16,1,4096]{2,1,0:T(1,128)} reshape(f32[256,1,2,2,4,16]{5,4,3,2,1,0:T(4,128)S(1)} %bitcast.117) | data formatting | bytes 524288
  139.6 9.8 %all-to-all-start.1 = ((f32[16,1,4096]{2,1,0:T(1,128)}), f32[16,1,4096]{2,1,0:T(1,128)S(1)}, u32[]{:S(2)}, u32[]{:S(2)}) async-start(f32[16,1,4096]{2,1,0:T(1,128)} %reshape.340), calls=%async_computation.1 | async-start | bytes 524288 | tf_op jit(solution)/shard_map/all_to_all | solution.py:156
  149.4 1.1 sine_multiply_fusion
  150.6 1.4 fusion.95
  152.0 10.0 %all-to-all-done.1 = f32[16,1,4096]{2,1,0:T(1,128)S(1)} async-done(((f32[16,1,4096]{2,1,0:T(1,128)}), f32[16,1,4096]{2,1,0:T(1,128)S(1)}, u32[]{:S(2)}, u32[]{:S(2)}) %all-to-all-start.1) | async-done | bytes 262176 | tf_op jit(solution)/shard_map/all_to_all | solution.py:156
  162.0 1.2 reduce.1
  163.2 1.5 reshape.341
  164.8 2.6 %copy.44 = f32[2,1,4,2,16,16,16]{6,4,5,3,2,0,1:T(8,128)} copy(f32[2,1,4,2,16,16,16]{6,2,0,3,5,4,1:T(4,128)S(1)} %bitcast.118) | data formatting | bytes 524288 | tf_op jit(solution)/shard_map/all_to_all | solution.py:156
  167.4 2.6 %reshape.329 = f32[2,4,2,16,256]{4,3,2,1,0:T(8,128)S(1)} reshape(f32[2,1,4,2,16,16,16]{6,5,4,3,2,0,1:T(8,128)} %bitcast.119) | data formatting | bytes 524288 | tf_op jit(solution)/shard_map/reshape.33
  170.0 0.7 convolution_bitcast_fusion.3
  171.1 0.9 multiply_add_fusion
  (87 shorter events, 4.4 us)
Async XLA Ops:
  2.7 3.8 %copy-start.1 = (f32[256,1,256]{2,0,1:T(8,128)}, f32[256,1,256]{2,0,1:T(8,128)S(1)}, u32[]{:S(2)}) copy-start(f32[256,1,256]{2,0,1:T(8,128)S(1)} %fusion.39) | copy-start | bytes 786436
  3.8 0.7 copy-start.4
  5.1 0.8 copy-start.9
  5.1 0.8 copy-start.11
  5.9 0.7 copy-start.7
  13.0 17.4 %copy-start.22 = (f32[6,4,16,8]{2,3,1,0:T(8,128)S(1)}, f32[6,4,16,8]{2,3,1,0:T(8,128)}, u32[]{:S(2)}) copy-start(f32[6,4,16,8]{2,3,1,0:T(8,128)} %param.5) | copy-start | bytes 36868
  20.2 91.2 %all-to-all-start = ((f32[16,1,12288]{2,1,0:T(1,128)}), f32[16,1,12288]{2,1,0:T(1,128)S(1)}, u32[]{:S(2)}, u32[]{:S(2)}) async-start(f32[16,1,12288]{2,1,0:T(1,128)} %reshape.338), calls=%async_computation | async-start | bytes 1572864 | tf_op jit(solution)/shard_map/all_to_all | solution.py:86
  129.7 5.8 %copy-start.13 = (f32[1,4,16,256]{3,2,1,0:T(8,128)S(1)}, f32[1,4,16,256]{3,2,1,0:T(8,128)}, u32[]{:S(2)}) copy-start(f32[1,4,16,256]{3,2,1,0:T(8,128)} %copy.35) | copy-start | bytes 196612
  129.7 5.8 %copy-start.14 = (f32[1,4,16,256]{3,2,1,0:T(8,128)S(1)}, f32[1,4,16,256]{3,2,1,0:T(8,128)}, u32[]{:S(2)}) copy-start(f32[1,4,16,256]{3,2,1,0:T(8,128)} %copy.36) | copy-start | bytes 196612
  129.7 5.8 %copy-start.15 = (f32[1,4,16,256]{3,2,1,0:T(8,128)S(1)}, f32[1,4,16,256]{3,2,1,0:T(8,128)}, u32[]{:S(2)}) copy-start(f32[1,4,16,256]{3,2,1,0:T(8,128)} %copy.37) | copy-start | bytes 196612
  129.7 5.8 %copy-start.16 = (f32[1,4,16,256]{3,2,1,0:T(8,128)S(1)}, f32[1,4,16,256]{3,2,1,0:T(8,128)}, u32[]{:S(2)}) copy-start(f32[1,4,16,256]{3,2,1,0:T(8,128)} %copy.38) | copy-start | bytes 196612
  129.7 5.9 %copy-start.2 = (f32[256,1,256]{2,0,1:T(8,128)S(1)}, f32[256,1,256]{2,0,1:T(8,128)}, u32[]{:S(2)}) copy-start(f32[256,1,256]{2,0,1:T(8,128)} %copy-done.1) | copy-start | bytes 786436
  136.0 14.4 %copy-start.3 = (f32[256,256]{1,0:T(8,128)S(1)}, f32[256,256]{1,0:T(8,128)}, u32[]{:S(2)}) copy-start(f32[256,256]{1,0:T(8,128)} %fusion.40) | copy-start | bytes 786436
  139.6 22.4 %all-to-all-start.1 = ((f32[16,1,4096]{2,1,0:T(1,128)}), f32[16,1,4096]{2,1,0:T(1,128)S(1)}, u32[]{:S(2)}, u32[]{:S(2)}) async-start(f32[16,1,4096]{2,1,0:T(1,128)} %reshape.340), calls=%async_computation.1 | async-start | bytes 524288 | tf_op jit(solution)/shard_map/all_to_all | solution.py:156
  164.7 6.0 %copy-start.8 = (f32[1,4,16,256]{3,2,1,0:T(8,128)S(1)}, f32[1,4,16,256]{3,2,1,0:T(8,128)}, u32[]{:S(2)}) copy-start(f32[1,4,16,256]{3,2,1,0:T(8,128)} %copy-done.7) | copy-start | bytes 196612
  164.7 6.0 %copy-start.12 = (f32[1,4,16,256]{3,2,1,0:T(8,128)S(1)}, f32[1,4,16,256]{3,2,1,0:T(8,128)}, u32[]{:S(2)}) copy-start(f32[1,4,16,256]{3,2,1,0:T(8,128)} %copy-done.11) | copy-start | bytes 196612
  164.7 6.0 %copy-start.19 = (f32[1,4,16,256]{3,2,1,0:T(8,128)S(1)}, f32[1,4,16,256]{3,2,1,0:T(8,128)}, u32[]{:S(2)}) copy-start(f32[1,4,16,256]{3,2,1,0:T(8,128)} %get-tuple-element.29) | copy-start | bytes 196612
  164.7 6.0 %copy-start.21 = (f32[1,4,16,256]{3,2,1,0:T(8,128)S(1)}, f32[1,4,16,256]{3,2,1,0:T(8,128)}, u32[]{:S(2)}) copy-start(f32[1,4,16,256]{3,2,1,0:T(8,128)} %get-tuple-element.38) | copy-start | bytes 196612
  164.8 6.0 %copy-start.27 = (f32[1,1,16,256]{3,2,1,0:T(8,128)S(1)}, f32[1,1,16,256]{3,2,1,0:T(8,128)}, u32[]{:S(2)}) copy-start(f32[1,1,16,256]{3,2,1,0:T(8,128)} %get-tuple-element.31) | copy-start | bytes 49156
  164.8 6.0 %copy-start.28 = (f32[1,1,16,256]{3,2,1,0:T(8,128)S(1)}, f32[1,1,16,256]{3,2,1,0:T(8,128)}, u32[]{:S(2)}) copy-start(f32[1,1,16,256]{3,2,1,0:T(8,128)} %get-tuple-element.32) | copy-start | bytes 49156
  164.8 6.0 %copy-start.29 = (f32[1,1,16,256]{3,2,1,0:T(8,128)S(1)}, f32[1,1,16,256]{3,2,1,0:T(8,128)}, u32[]{:S(2)}) copy-start(f32[1,1,16,256]{3,2,1,0:T(8,128)} %get-tuple-element.48) | copy-start | bytes 49156
  164.8 6.0 %copy-start.30 = (f32[1,1,16,256]{3,2,1,0:T(8,128)S(1)}, f32[1,1,16,256]{3,2,1,0:T(8,128)}, u32[]{:S(2)}) copy-start(f32[1,1,16,256]{3,2,1,0:T(8,128)} %get-tuple-element.51) | copy-start | bytes 49156
  167.4 3.5 %copy-start.6 = (f32[1,4,16,256]{3,2,1,0:T(8,128)S(1)}, f32[1,4,16,256]{3,2,1,0:T(8,128)}, u32[]{:S(2)}) copy-start(f32[1,4,16,256]{3,2,1,0:T(8,128)} %copy-done.5) | copy-start | bytes 196612
  167.4 3.5 %copy-start.10 = (f32[1,4,16,256]{3,2,1,0:T(8,128)S(1)}, f32[1,4,16,256]{3,2,1,0:T(8,128)}, u32[]{:S(2)}) copy-start(f32[1,4,16,256]{3,2,1,0:T(8,128)} %copy-done.9) | copy-start | bytes 196612
  167.4 3.5 %copy-start.18 = (f32[1,4,16,256]{3,2,1,0:T(8,128)S(1)}, f32[1,4,16,256]{3,2,1,0:T(8,128)}, u32[]{:S(2)}) copy-start(f32[1,4,16,256]{3,2,1,0:T(8,128)} %get-tuple-element.28) | copy-start | bytes 196612
  167.4 3.5 %copy-start.20 = (f32[1,4,16,256]{3,2,1,0:T(8,128)S(1)}, f32[1,4,16,256]{3,2,1,0:T(8,128)}, u32[]{:S(2)}) copy-start(f32[1,4,16,256]{3,2,1,0:T(8,128)} %get-tuple-element.43) | copy-start | bytes 196612
  167.4 3.6 %copy-start.23 = (f32[1,1,16,256]{3,2,1,0:T(8,128)S(1)}, f32[1,1,16,256]{3,2,1,0:T(8,128)}, u32[]{:S(2)}) copy-start(f32[1,1,16,256]{3,2,1,0:T(8,128)} %get-tuple-element.30) | copy-start | bytes 49156
  167.4 3.6 %copy-start.24 = (f32[1,1,16,256]{3,2,1,0:T(8,128)S(1)}, f32[1,1,16,256]{3,2,1,0:T(8,128)}, u32[]{:S(2)}) copy-start(f32[1,1,16,256]{3,2,1,0:T(8,128)} %get-tuple-element.33) | copy-start | bytes 49156
  167.4 3.6 %copy-start.25 = (f32[1,1,16,256]{3,2,1,0:T(8,128)S(1)}, f32[1,1,16,256]{3,2,1,0:T(8,128)}, u32[]{:S(2)}) copy-start(f32[1,1,16,256]{3,2,1,0:T(8,128)} %get-tuple-element.49) | copy-start | bytes 49156
  167.4 3.6 %copy-start.26 = (f32[1,1,16,256]{3,2,1,0:T(8,128)S(1)}, f32[1,1,16,256]{3,2,1,0:T(8,128)}, u32[]{:S(2)}) copy-start(f32[1,1,16,256]{3,2,1,0:T(8,128)} %get-tuple-element.50) | copy-start | bytes 49156
  167.4 3.6 %copy-start = (f32[2,1,4,16,512]{4,3,2,1,0:T(8,128)S(1)}, f32[2,1,4,16,512]{4,3,2,1,0:T(8,128)}, u32[]{:S(2)}) copy-start(f32[2,1,4,16,512]{4,3,2,1,0:T(8,128)} %param.3) | copy-start | bytes 786436
  167.4 3.6 %copy-start.17 = (f32[2,1,4,16,512]{4,3,2,1,0:T(8,128)S(1)}, f32[2,1,4,16,512]{4,3,2,1,0:T(8,128)}, u32[]{:S(2)}) copy-start(f32[2,1,4,16,512]{4,3,2,1,0:T(8,128)} %param.4) | copy-start | bytes 786436
  (1 other events, 0.6 us)
where the time goes:
time: 173 us; the launch traced here: 172 us
  blocking collectives  71 us (41%)
  local copies, waits for them, and re-layouts  54.2 us (31%)
  starting transfers between devices  20 us (12%)
  other arithmetic  12.2 us (7%)
  waiting for transfers between devices  10 us (6%)
  matrix products  3.41 us (2%)
    all_gather x1, blocking collectives, on_device(): base_all = lax.all_gather(base_flow, 'ens', axis=3, tiled=True)  71 us
    unnamed x73, local copies, waits for them, and re-layouts  24.2 us
    all_to_all x1, starting transfers between devices, to_physical(): lax.all_to_all(mixed_space, 'pen', split_axis=4, concat_axis=5, tiled=True)  10.2 us
    all_to_all x1, waiting for transfers between devices, on_device(): lax.all_to_all(spread, 'pen', split_axis=4, concat_axis=5, tiled=True)  10 us
    all_to_all x1, starting transfers between devices, on_device(): lax.all_to_all(spread, 'pen', split_axis=4, concat_axis=5, tiled=True)  9.75 us
    all_to_all x2, local copies, waits for them, and re-layouts, to_physical(): lax.all_to_all(mixed_space, 'pen', split_axis=4, concat_axis=5, tiled=True)  9.59 us
    another operation x2, local copies, waits for them, and re-layouts  7.5 us
    transpose x1, local copies, waits for them, and re-layouts, to_physical(): jnp.einsum('fplkj,jcx->fplcxk', spectral, x_table, precision=lax.Precisio...  4.97 us
  transfers between devices with their start and end apart: 2, of which 1 were waited for; matrix products, arithmetic and copies ran while one was open for 7% of the time, Pallas kernels for 0%

commit v1 on v0

--- a/solution.py
+++ b/solution.py
@@ -153,7 +153,10 @@
     )
     spectra = jnp.einsum(
         "fplckx,cxm->fplkm",
-        lax.all_to_all(spread, "pen", split_axis=4, concat_axis=5, tiled=True),
+        jnp.concatenate(
+            lax.all_to_all(jnp.stack(jnp.split(spread, lax.axis_size("pen"), axis=4)), "pen", 0, 0),
+            axis=5,
+        ),
         x_forward,
         precision=lax.Precision.HIGHEST,
     )

time: 173 us -> 171 us (0.988)
  local copies, waits for them, and re-layouts: 54.2 us -> 50.6 us
    reshape x0 -> x2, local copies, waits for them, and re-layouts: none -> 3.7 us  [on_device(): jnp.concatenate(lax.all_to_all(jnp.stack(jnp.split(spread, lax.axis_size(...]
    all_to_all x1 -> x0, local copies, waits for them, and re-layouts: 2.57 us -> none  [on_device(): lax.all_to_all(spread, 'pen', split_axis=4, concat_axis=5, tiled=True)]
    another operation x2 -> x3, local copies, waits for them, and re-layouts: 7.5 us -> 5.94 us
    unnamed x73 -> x74, local copies, waits for them, and re-layouts: 24.2 us -> 23.3 us
where the time goes in v1:
time: 171 us; the launch traced here: 170 us
  blocking collectives  71 us (42%)
  local copies, waits for them, and re-layouts  50.6 us (30%)
  starting transfers between devices  20.1 us (12%)
  other arithmetic  13.2 us (8%)
  waiting for transfers between devices  10.8 us (6%)
  matrix products  3.41 us (2%)
    all_gather x1, blocking collectives, on_device(): base_all = lax.all_gather(base_flow, 'ens', axis=3, tiled=True)  71 us
    unnamed x74, local copies, waits for them, and re-layouts  23.3 us
    all_to_all x1, waiting for transfers between devices, on_device(): lax.all_to_all(jnp.stack(jnp.split(spread, lax.axis_size('pen'), axis=4))...  10.8 us
    all_to_all x1, starting transfers between devices, to_physical(): lax.all_to_all(mixed_space, 'pen', split_axis=4, concat_axis=5, tiled=True)  10.2 us
    all_to_all x1, starting transfers between devices, on_device(): lax.all_to_all(jnp.stack(jnp.split(spread, lax.axis_size('pen'), axis=4))...  9.88 us
    all_to_all x2, local copies, waits for them, and re-layouts, to_physical(): lax.all_to_all(mixed_space, 'pen', split_axis=4, concat_axis=5, tiled=True)  9.55 us
    another operation x2, local copies, waits for them, and re-layouts  5.84 us
    transpose x1, local copies, waits for them, and re-layouts, to_physical(): jnp.einsum('fplkj,jcx->fplcxk', spectral, x_table, precision=lax.Precisio...  4.95 us
  transfers between devices with their start and end apart: 2, of which 1 were waited for; matrix products, arithmetic and copies ran while one was open for 7% of the time, Pallas kernels for 0%

profile of v1, /device:TPU:1, one launch (start us, length us, event | category | flops | bytes accessed | tf_op | source)
XLA Modules:
  0.0 170.4 jit_solution(15799575634628017590)
XLA Ops:
  0.7 1.1 sine_multiply_fusion.1
  1.7 1.0 fusion.55
  2.7 1.1 slice_bitcast_fusion.17
  5.2 0.7 fusion.89
  6.5 1.5 convolution_bitcast_fusion
  8.0 4.9 %copy.27 = f32[6,1,4,2,256,16]{5,2,0,3,1,4:T(4,128)} copy(f32[6,1,4,2,256,16]{4,5,2,0,3,1:T(8,128)S(1)} %convolution_bitcast_fusion) | data formatting | bytes 1572864 | tf_op jit(solution)/shard_map/fplkj,jcx->fplcxk/transpose | solution.py:81
  12.9 7.2 %reshape.343 = f32[16,1,12288]{2,1,0:T(1,128)} reshape(f32[256,1,2,6,4,16]{5,4,3,2,1,0:T(4,128)} %bitcast.177) | data formatting | bytes 1572864
  20.2 10.2 %all-to-all-start = ((f32[16,1,12288]{2,1,0:T(1,128)}), f32[16,1,12288]{2,1,0:T(1,128)S(1)}, u32[]{:S(2)}, u32[]{:S(2)}) async-start(f32[16,1,12288]{2,1,0:T(1,128)} %reshape.343), calls=%async_computation | async-start | bytes 1572864 | tf_op jit(solution)/shard_map/all_to_all | solution.py:86
  30.4 71.0 %all_gather.3 = f32[6,4,16,256]{2,1,0,3:T(4,128)S(1)} all-gather(f32[6,4,16,8]{2,1,0,3:T(4,128)S(1)} %copy.20), channel_id=1, replica_groups=mesh['ens'=32,'pen'=16] {'ens'}, dimensions={3}, use_global_device_ids=true | all-gather | bytes 405504 | tf_op jit(solution)/shard_map/all_gather | solution.py:95
  101.4 1.5 fusion.110
  102.9 1.8 %copy.41 = f32[1,4,16,256]{3,2,1,0:T(8,128)} copy(f32[1,4,16,256]{2,1,0,3:T(4,128)} %get-tuple-element.8) | data formatting | bytes 131072
  104.7 1.8 %copy.42 = f32[1,4,16,256]{3,2,1,0:T(8,128)} copy(f32[1,4,16,256]{2,1,0,3:T(4,128)} %get-tuple-element.7) | data formatting | bytes 131072
  106.6 0.8 copy.43
  107.9 1.7 fusion.56
  109.6 1.1 multiply_negate_fusion
  111.2 2.4 %reduce = f32[16,12288]{1,0:T(8,128)S(1)} reduce(f32[16,1,12288]{2,1,0:T(1,128)S(1)} %all-to-all-done, f32[]{:T(128)} %broadcast.510), dimensions={1}, to_apply=%all_to_all.14.reduce_sub_computation | reduce | bytes 1572868 | tf_op jit(solution)/shard_map/all_to_all | solution.py:86
  113.7 6.3 %reshape.344 = f32[256,1,2,6,4,16]{5,4,3,2,1,0:T(4,128)} reshape(f32[16,12288]{1,0:T(8,128)S(1)} %reduce) | data formatting | bytes 1572864
  120.0 9.1 %copy.48 = f32[6,1,4,2,16,16,16]{6,4,5,3,2,0,1:T(8,128)} copy(f32[6,1,4,2,16,16,16]{6,2,0,3,5,4,1:T(4,128)} %bitcast.178) | data formatting | bytes 1572864 | tf_op jit(solution)/shard_map/all_to_all | solution.py:86
  129.0 4.9 %reshape.331 = f32[6,4,2,16,256]{4,3,2,1,0:T(8,128)S(1)} reshape(f32[6,1,4,2,16,16,16]{6,5,4,3,2,0,1:T(8,128)} %bitcast.179) | data formatting | bytes 1572864 | tf_op jit(solution)/shard_map/reshape.18
  134.0 0.8 convolution_bitcast_fusion.1
  136.8 1.5 reshape.345
  138.3 9.9 %all-to-all-start.1 = ((f32[16,1,4096]{2,1,0:T(1,128)}), f32[16,1,4096]{2,1,0:T(1,128)S(1)}, u32[]{:S(2)}, u32[]{:S(2)}) async-start(f32[16,1,4096]{2,1,0:T(1,128)} %reshape.345), calls=%async_computation.1 | async-start | bytes 524288 | tf_op jit(solution)/shard_map/all_to_all | solution.py:157
  148.2 1.1 sine_multiply_fusion
  150.0 10.8 %all-to-all-done.1 = f32[16,1,4096]{2,1,0:T(1,128)S(1)} async-done(((f32[16,1,4096]{2,1,0:T(1,128)}), f32[16,1,4096]{2,1,0:T(1,128)S(1)}, u32[]{:S(2)}, u32[]{:S(2)}) %all-to-all-start.1) | async-done | bytes 262176 | tf_op jit(solution)/shard_map/all_to_all | solution.py:157
  160.8 1.2 reduce.1
  162.0 0.7 reshape.346
  162.7 1.5 bitcast_bitcast_fusion
  164.2 2.2 %copy.34 = f32[2,1,4,2,16,16,16]{6,5,4,3,2,0,1:T(8,128)S(1)} copy(f32[2,1,4,2,16,16,16]{4,6,2,0,3,1,5:T(8,128)} %bitcast_bitcast_fusion) | data formatting | bytes 524288 | tf_op jit(solution)/shard_map/reshape | solution.py:156
  166.5 0.9 reshape.334
  167.5 0.7 convolution_bitcast_fusion.3
  168.2 1.1 fusion.72
  169.5 0.9 multiply_add_fusion
  (89 shorter events, 5.8 us)
Async XLA Ops:
  2.7 3.8 %copy-start.1 = (f32[256,1,256]{2,0,1:T(8,128)}, f32[256,1,256]{2,0,1:T(8,128)S(1)}, u32[]{:S(2)}) copy-start(f32[256,1,256]{2,0,1:T(8,128)S(1)} %fusion.55) | copy-start | bytes 786436
  3.8 0.7 copy-start.4
  5.1 0.8 copy-start.10
  5.1 0.8 copy-start.12
  5.9 0.6 copy-start.6
  5.9 0.7 copy-start.8
  12.9 17.4 %copy-start.19 = (f32[6,4,16,8]{2,3,1,0:T(8,128)S(1)}, f32[6,4,16,8]{2,3,1,0:T(8,128)}, u32[]{:S(2)}) copy-start(f32[6,4,16,8]{2,3,1,0:T(8,128)} %param.5) | copy-start | bytes 36868
  20.2 90.5 %all-to-all-start = ((f32[16,1,12288]{2,1,0:T(1,128)}), f32[16,1,12288]{2,1,0:T(1,128)S(1)}, u32[]{:S(2)}, u32[]{:S(2)}) async-start(f32[16,1,12288]{2,1,0:T(1,128)} %reshape.343), calls=%async_computation | async-start | bytes 1572864 | tf_op jit(solution)/shard_map/all_to_all | solution.py:86
  129.0 5.7 %copy-start.13 = (f32[1,4,16,256]{3,2,1,0:T(8,128)S(1)}, f32[1,4,16,256]{3,2,1,0:T(8,128)}, u32[]{:S(2)}) copy-start(f32[1,4,16,256]{3,2,1,0:T(8,128)} %copy.41) | copy-start | bytes 196612
  129.0 5.7 %copy-start.14 = (f32[1,4,16,256]{3,2,1,0:T(8,128)S(1)}, f32[1,4,16,256]{3,2,1,0:T(8,128)}, u32[]{:S(2)}) copy-start(f32[1,4,16,256]{3,2,1,0:T(8,128)} %copy.42) | copy-start | bytes 196612
  129.0 5.7 %copy-start.15 = (f32[1,4,16,256]{3,2,1,0:T(8,128)S(1)}, f32[1,4,16,256]{3,2,1,0:T(8,128)}, u32[]{:S(2)}) copy-start(f32[1,4,16,256]{3,2,1,0:T(8,128)} %copy.43) | copy-start | bytes 196612
  133.9 1.0 copy-start.2
  136.5 12.7 %copy-start.3 = (f32[256,256]{1,0:T(8,128)S(1)}, f32[256,256]{1,0:T(8,128)}, u32[]{:S(2)}) copy-start(f32[256,256]{1,0:T(8,128)} %fusion.56) | copy-start | bytes 786436
  138.3 11.1 %copy-start.5 = (f32[1,4,16,512]{3,2,1,0:T(8,128)S(1)}, f32[1,4,16,512]{3,2,1,0:T(8,128)}, u32[]{:S(2)}) copy-start(f32[1,4,16,512]{3,2,1,0:T(8,128)} %copy-done.4) | copy-start | bytes 393220
  138.3 22.5 %all-to-all-start.1 = ((f32[16,1,4096]{2,1,0:T(1,128)}), f32[16,1,4096]{2,1,0:T(1,128)S(1)}, u32[]{:S(2)}, u32[]{:S(2)}) async-start(f32[16,1,4096]{2,1,0:T(1,128)} %reshape.345), calls=%async_computation.1 | async-start | bytes 524288 | tf_op jit(solution)/shard_map/all_to_all | solution.py:157
  166.4 1.8 %copy-start.9 = (f32[1,4,16,256]{3,2,1,0:T(8,128)S(1)}, f32[1,4,16,256]{3,2,1,0:T(8,128)}, u32[]{:S(2)}) copy-start(f32[1,4,16,256]{3,2,1,0:T(8,128)} %copy-done.8) | copy-start | bytes 196612
  166.5 2.8 %copy-start.7 = (f32[1,4,16,256]{3,2,1,0:T(8,128)S(1)}, f32[1,4,16,256]{3,2,1,0:T(8,128)}, u32[]{:S(2)}) copy-start(f32[1,4,16,256]{3,2,1,0:T(8,128)} %copy-done.6) | copy-start | bytes 196612
  167.4 1.9 %copy-start.11 = (f32[1,4,16,256]{3,2,1,0:T(8,128)S(1)}, f32[1,4,16,256]{3,2,1,0:T(8,128)}, u32[]{:S(2)}) copy-start(f32[1,4,16,256]{3,2,1,0:T(8,128)} %copy-done.10) | copy-start | bytes 196612
  167.4 1.9 %copy-start.17 = (f32[1,4,16,256]{3,2,1,0:T(8,128)S(1)}, f32[1,4,16,256]{3,2,1,0:T(8,128)}, u32[]{:S(2)}) copy-start(f32[1,4,16,256]{3,2,1,0:T(8,128)} %get-tuple-element.28) | copy-start | bytes 196612
  167.4 1.9 %copy-start.18 = (f32[1,4,16,256]{3,2,1,0:T(8,128)S(1)}, f32[1,4,16,256]{3,2,1,0:T(8,128)}, u32[]{:S(2)}) copy-start(f32[1,4,16,256]{3,2,1,0:T(8,128)} %get-tuple-element.43) | copy-start | bytes 196612
  167.4 1.9 %copy-start.20 = (f32[1,1,16,256]{3,2,1,0:T(8,128)S(1)}, f32[1,1,16,256]{3,2,1,0:T(8,128)}, u32[]{:S(2)}) copy-start(f32[1,1,16,256]{3,2,1,0:T(8,128)} %get-tuple-element.30) | copy-start | bytes 49156
  167.4 1.9 %copy-start.21 = (f32[1,1,16,256]{3,2,1,0:T(8,128)S(1)}, f32[1,1,16,256]{3,2,1,0:T(8,128)}, u32[]{:S(2)}) copy-start(f32[1,1,16,256]{3,2,1,0:T(8,128)} %get-tuple-element.33) | copy-start | bytes 49156
  167.5 1.9 %copy-start.22 = (f32[1,1,16,256]{3,2,1,0:T(8,128)S(1)}, f32[1,1,16,256]{3,2,1,0:T(8,128)}, u32[]{:S(2)}) copy-start(f32[1,1,16,256]{3,2,1,0:T(8,128)} %get-tuple-element.49) | copy-start | bytes 49156
  167.5 1.9 %copy-start.23 = (f32[1,1,16,256]{3,2,1,0:T(8,128)S(1)}, f32[1,1,16,256]{3,2,1,0:T(8,128)}, u32[]{:S(2)}) copy-start(f32[1,1,16,256]{3,2,1,0:T(8,128)} %get-tuple-element.50) | copy-start | bytes 49156
  167.5 2.0 %copy-start = (f32[2,1,4,16,512]{4,3,2,1,0:T(8,128)S(1)}, f32[2,1,4,16,512]{4,3,2,1,0:T(8,128)}, u32[]{:S(2)}) copy-start(f32[2,1,4,16,512]{4,3,2,1,0:T(8,128)} %param.3) | copy-start | bytes 786436
  167.5 2.0 %copy-start.16 = (f32[2,1,4,16,512]{4,3,2,1,0:T(8,128)S(1)}, f32[2,1,4,16,512]{4,3,2,1,0:T(8,128)}, u32[]{:S(2)}) copy-start(f32[2,1,4,16,512]{4,3,2,1,0:T(8,128)} %param.4) | copy-start | bytes 786436
